TPU v7x, 32 devices: a whole 2x2x4 slice. The times are simulated.
32 devices in a mesh: groups: 2 (over x), gx: 16 (over z, y, core).
Axes of the slice: x: 2, y: 2, z: 4, core: 2. Of those that a mesh axis runs over, the one named last changes fastest.
Arguments:
- features: bfloat16 [128, 8, 8, 8, 128], P(('groups', 'gx')), parts along dimension 0, may hold values from -6 to 6
- fine_nbr: int32 [128, 27], P(('groups', 'gx')), parts along dimension 0, may hold values from -1 to 3, as said below
- fine_send: int32 [32, 2, 4], P(('groups', 'gx')), parts along dimension 0, may hold values from -1 to 3, as said below
- fine_parent: int32 [128], P(('groups', 'gx')), parts along dimension 0, may hold values from -1 to 127, as said below
- coarse_child: int32 [32, 8], P(('groups', 'gx')), parts along dimension 0, may hold values from -1 to 63, as said below
- coarse_nbr: int32 [32, 27], P(('groups', 'gx')), parts along dimension 0, may hold values from -1 to 15, as said below
- enc_fine_w: bfloat16 [27, 128, 128], replicated, may hold values from -0.15625 to 0.15625
- enc_coarse_w: bfloat16 [27, 128, 128], replicated, may hold values from -0.15625 to 0.15625
- dec_coarse_w: bfloat16 [27, 128, 128], replicated, may hold values from -0.15625 to 0.15625
- dec_fine_w: bfloat16 [27, 128, 128], replicated, may hold values from -0.15625 to 0.15625
Outputs:
- fine_out: bfloat16 [128, 8, 8, 8, 128], P(('groups', 'gx')), parts along dimension 0
There are 2 independent parts, one for each index of `groups`. A program takes and returns all parts, laid end to end along the dimension named above; an argument that names none is the same for every part. Nothing has to cross between parts.
Inputs may be any that keep to these rules, and one draw needn't show every extreme that they name: `fine_nbr`: entry t of a fine slot on gx device d names the slot, on device d + dx, of the brick at brick offset (dx, dy, dz), or is -1 where there is none. A slot whose entry 13 is -1 holds no brick and all its entries are -1; entry 13 of a brick is its own slot. Adjacency is symmetric. `fine_send`: on device d, entry s of row 0 is s when slot s holds a brick with a neighbour on device d + 1, else -1; row 1 likewise for device d - 1. `fine_parent`: 8 g + o for a brick whose parent is coarse slot g at octant o, -1 for slots without a brick. Coarse slot g is held by gx device g, which lies in the same aligned group of four gx devices as the child's device. `coarse_child`: entry o of coarse slot g is the fine slot f with fine_parent[f] = 8 g + o, or -1 where there is none. `coarse_nbr`: entry t (taps ordered as for fine_nbr) is the coarse slot of the neighbouring coarse brick, or -1 where there is none; entry 13 is the brick's own slot; every neighbour is held by a gx device of the same or an adjacent aligned group of four, and neighbours with dx = 0 by a device of the same aligned group of four.
All inputs are finite; a program needn't handle non-finite values.
Results may differ from a plain program's by a relative error of at most 0.01.
Values may be sent and summed in bfloat16 or wider, within the bound.
A program may use at most 128 MiB of HBM per device.

v0:
```python
import functools

import jax
import jax.numpy as jnp
from jax import lax
from jax.experimental import pallas as pl
from jax.experimental.pallas import tpu as pltpu
from jax.sharding import PartitionSpec as P

F32 = jnp.float32
BF16 = jnp.bfloat16
LANES = 4
MESH = pl.DeviceIdType.MESH


def pick(offset, edge):
    if offset < 0:
        return slice(edge - 1, edge)
    if offset == 0:
        return slice(0, edge)
    return slice(0, 1)


def place(offset, edge, base):
    if offset < 0:
        return slice(base - 1, base)
    if offset == 0:
        return slice(base, base + edge)
    return slice(base + edge, base + edge + 1)


def kernel(
    n,
    fine_nbr,
    fine_send,
    fine_parent,
    child_ref,
    nbr_ref,
    feat_hbm,
    w1_hbm,
    w2_hbm,
    w3_hbm,
    w4_hbm,
    out_ref,
    feat,
    w1,
    w2,
    w3,
    w4,
    pad,
    cols,
    table,
    enc,
    below,
    above,
    face_out,
    face_in,
    face_out2,
    face_in2,
    half_z,
    pooled,
    children,
    meta,
    meta_s,
    coarse,
    coarse2,
    coarse3,
    low_x,
    high_x,
    side_out,
    side_in,
    side_out2,
    side_in2,
    spread,
    lifted,
    load_sem,
    face_send_sem,
    face_recv_sem,
    pool_send_sem,
    pool_recv_sem,
    meta_send_sem,
    meta_recv_sem,
    side_send_sem,
    side_recv_sem,
    meta_sem,
):
    slots, edge = out_ref.shape[0], enc.shape[1]
    plane = edge * edge
    width = out_ref.shape[-1]
    half = edge // 2
    block = half**3
    per = child_ref.shape[0]
    bricks = LANES * per
    me = lax.axis_index("gx")
    member = lax.rem(me, LANES)
    group = lax.div(me, LANES)

    def peer(k):
        return me - member + (member ^ k)

    loads = [
        pltpu.make_async_copy(src, dst, load_sem.at[i])
        for i, (src, dst) in enumerate(
            ((feat_hbm, feat), (w1_hbm, w1), (w2_hbm, w2), (w3_hbm, w3), (w4_hbm, w4))
        )
    ]
    for copy in loads:
        copy.start()

    has_prev, has_next = me > 0, me < n - 1
    has_down, has_up = me >= LANES, me < n - LANES
    barrier = pltpu.get_barrier_semaphore()

    def greet(other):
        pl.semaphore_signal(barrier, inc=1, device_id={"gx": other}, device_id_type=MESH)

    sides = (
        (has_prev & (member == 0), me - 1),
        (has_next & (member == LANES - 1), me + 1),
        (has_down, me - LANES),
        (has_up, me + LANES),
    )
    for k in range(1, LANES):
        greet(peer(k))
    peers = LANES - 1
    for there, other in sides:
        pl.when(there)(functools.partial(greet, other))
        peers = peers + jnp.where(there, 1, 0)
    pl.semaphore_wait(barrier, peers)

    def remote(src, dst, send, recv, other):
        return pltpu.make_async_remote_copy(
            src_ref=src,
            dst_ref=dst,
            send_sem=send,
            recv_sem=recv,
            device_id={"gx": other},
            device_id_type=MESH,
        )

    def face_copies(outgoing, incoming, phase):
        up = remote(
            outgoing.at[0],
            incoming.at[0],
            face_send_sem.at[phase, 0],
            face_recv_sem.at[phase, 0],
            me + 1,
        )
        down = remote(
            outgoing.at[1],
            incoming.at[1],
            face_send_sem.at[phase, 1],
            face_recv_sem.at[phase, 1],
            me - 1,
        )
        return up, down

    def start_pair(up, up_there, down, down_there):
        pl.when(up_there)(up.start)
        pl.when(down_there)(down.start)

    def finish_pair(up, up_there, down, down_there):
        @pl.when(down_there)
        def _():
            up.wait_recv()
            down.wait_send()

        @pl.when(up_there)
        def _():
            down.wait_recv()
            up.wait_send()

    meta[member, 0:per, 0 : child_ref.shape[1]] = child_ref[...]
    meta[member, per : 2 * per, 0 : nbr_ref.shape[1]] = nbr_ref[...]

    cube = (edge, edge, edge, width)
    zero_brick = jnp.zeros(cube, F32)
    zero_plane = jnp.zeros((edge, edge, width), F32)
    table[slots] = zero_brick

    def stage_faces(outgoing, s):
        up_from = jnp.where(fine_send[0, s] >= 0, s, slots)
        down_from = jnp.where(fine_send[1, s] >= 0, s, slots)
        outgoing[0, s] = table[up_from, edge - 1].reshape(plane, width).astype(BF16)
        outgoing[1, s] = table[down_from, 0].reshape(plane, width).astype(BF16)

    loads[0].wait()
    for s in range(slots):
        table[s] = feat[s].astype(F32).reshape(cube)
    for s in range(slots):
        stage_faces(face_out, s)
    halo1 = face_copies(face_out, face_in, 0)
    start_pair(halo1[0], has_next, halo1[1], has_prev)
    meta_copies = [
        remote(
            meta.at[member],
            meta.at[member],
            meta_send_sem.at[k - 1],
            meta_recv_sem.at[k - 1],
            peer(k),
        )
        for k in range(1, LANES)
    ]
    for copy in meta_copies:
        copy.start()

    below[slots] = zero_plane
    above[slots] = zero_plane
    coarse[bricks] = zero_brick
    coarse2[bricks] = zero_brick
    coarse3[bricks] = zero_brick
    low_x[3 * bricks] = zero_plane
    high_x[3 * bricks] = zero_plane
    children[LANES * slots] = jnp.zeros((block, width), F32)

    base = edge

    def convolve(centre, lower, upper, index, weights):
        for t in range(27):
            dx, dy, dz = t // 9 - 1, t // 3 % 3 - 1, t % 3 - 1
            at = index(t)
            ys, zs = pick(dy, edge), pick(dz, edge)
            if dx == 0:
                piece = centre[at, :, ys, zs, :]
            elif dx < 0:
                piece = lower[at, ys, zs, :][None]
            else:
                piece = upper[at, ys, zs, :][None]
            pad[place(dx, edge, 1), place(dy, edge, 1), place(dz, edge, base), :] = piece
        for x in range(edge + 2):
            for k in range(9):
                dy, dz = k // 3, k % 3 - 1
                piece = pad[x, dy : dy + edge, base + dz : base + dz + edge, :]
                cols[x * plane : (x + 1) * plane, k * width : (k + 1) * width] = piece.reshape(
                    plane, width
                ).astype(BF16)
        total = None
        for dx in range(3):
            part = jnp.dot(
                cols[dx * plane : (dx + edge) * plane, :],
                weights[dx],
                preferred_element_type=F32,
            )
            total = part if total is None else total + part
        return jnp.maximum(total, 0.0).astype(BF16)

    def fine_index(b):
        def index(t):
            at = fine_nbr[b, t]
            return jnp.where(at >= 0, at, slots)

        return index

    def take_faces(incoming):
        for s in range(slots):
            below[s] = incoming[0, s].astype(F32).reshape(edge, edge, width)
            above[s] = incoming[1, s].astype(F32).reshape(edge, edge, width)

    finish_pair(halo1[0], has_next, halo1[1], has_prev)
    take_faces(face_in)
    loads[1].wait()

    def pool_copy(k, b):
        return remote(
            pooled.at[member, b],
            pooled.at[member, b],
            pool_send_sem.at[k - 1, b],
            pool_recv_sem.at[k - 1, b],
            peer(k),
        )

    @pl.loop(0, slots)
    def _(b):
        value = convolve(table, below, above, fine_index(b), w1).astype(F32).reshape(cube)
        enc[b] = value
        pairs = value.reshape(half, 2, half, 2, edge, width)
        summed = (pairs[:, 0, :, 0] + pairs[:, 0, :, 1]) + (pairs[:, 1, :, 0] + pairs[:, 1, :, 1])
        half_z[...] = summed.reshape(half * half * edge, width)
        even = half_z[pl.ds(0, block, stride=2), :]
        odd = half_z[pl.ds(1, block, stride=2), :]
        pooled[member, b] = ((even + odd) * 0.125).astype(BF16)
        for k in range(1, LANES):
            pool_copy(k, b).start()

    for copy in meta_copies:
        copy.wait()
    to_smem = pltpu.make_async_copy(meta, meta_s, meta_sem)
    to_smem.start()
    for k in range(1, LANES):
        for b in range(slots):
            pool_copy(k, b).wait()
    to_smem.wait()
    for lane in range(LANES):
        for s in range(slots):
            children[lane * slots + s] = pooled[lane, s].astype(F32)

    def owner_of(value):
        value = jnp.maximum(value, 0)
        return lax.div(value, per), lax.rem(value, per)

    @pl.loop(0, bricks)
    def _(j):
        lane, slot = lax.div(j, per), lax.rem(j, per)
        for o in range(8):
            child = meta_s[lane, slot, o]
            safe = jnp.maximum(child, 0)
            at = lax.rem(lax.div(safe, slots), LANES) * slots + lax.rem(safe, slots)
            at = jnp.where(child >= 0, at, LANES * slots)
            ox, oy, oz = o // 4 * half, o // 2 % 2 * half, o % 2 * half
            for x in range(half):
                for y in range(half):
                    row = (x * half + y) * half
                    coarse[j, ox + x, oy + y, oz : oz + half, :] = children[
                        at, row : row + half, :
                    ]

    def side_copies(outgoing, incoming, phase):
        up = remote(
            outgoing,
            incoming.at[0],
            side_send_sem.at[phase, 0],
            side_recv_sem.at[phase, 0],
            me + LANES,
        )
        down = remote(
            outgoing,
            incoming.at[1],
            side_send_sem.at[phase, 1],
            side_recv_sem.at[phase, 1],
            me - LANES,
        )
        return up, down

    def coarse_index(j):
        lane, slot = lax.div(j, per), lax.rem(j, per)

        def index(t):
            value = meta_s[lane, per + slot, t]
            device, at = owner_of(value)
            at = lax.rem(device, LANES) * per + at
            if t // 9 == 1:
                return jnp.where(value >= 0, at, bricks)
            at = at + (lax.div(device, LANES) - group + 1) * bricks
            at = jnp.minimum(jnp.maximum(at, 0), 3 * bricks)
            return jnp.where(value >= 0, at, 3 * bricks)

        return index

    def coarse_layer(source, target, outgoing, incoming, phase, weights):
        for j in range(bricks):
            first, last = source[j, 0], source[j, edge - 1]
            low_x[bricks + j] = first
            high_x[bricks + j] = last
            outgoing[j, 0] = first.reshape(plane, width).astype(BF16)
            outgoing[j, 1] = last.reshape(plane, width).astype(BF16)
        up, down = side_copies(outgoing, incoming, phase)
        start_pair(up, has_up, down, has_down)
        finish_pair(up, has_up, down, has_down)
        for side, start in ((0, 0), (1, 2 * bricks)):
            for j in range(bricks):
                low_x[start + j] = incoming[side, j, 0].astype(F32).reshape(edge, edge, width)
                high_x[start + j] = incoming[side, j, 1].astype(F32).reshape(edge, edge, width)

        @pl.loop(0, bricks)
        def _(j):
            value = convolve(source, high_x, low_x, coarse_index(j), weights)
            target[j] = value.astype(F32).reshape(cube)

    loads[2].wait()
    coarse_layer(coarse, coarse2, side_out, side_in, 0, w2)
    loads[3].wait()
    coarse_layer(coarse2, coarse3, side_out2, side_in2, 1, w3)

    for s in range(slots):
        parent = fine_parent[s]
        safe = jnp.maximum(parent, 0)
        device, at = owner_of(lax.div(safe, 8))
        at = jnp.where(parent >= 0, lax.rem(device, LANES) * per + at, bricks)
        octant = lax.rem(safe, 8)
        ox = lax.div(octant, 4)
        oy = lax.rem(lax.div(octant, 2), 2)
        oz = lax.rem(octant, 2)
        piece = coarse3[at, pl.ds(ox * half, half), pl.ds(oy * half, half), :, :]
        piece = piece.reshape(half * half * edge, width)
        spread[pl.ds(0, half * half * edge, stride=2), :] = piece
        spread[pl.ds(1, half * half * edge, stride=2), :] = piece
        for z in range(2):
            for row in range(half * half):
                start = row * 2 * edge + z * edge
                lifted[z, row] = spread[start : start + edge, :]
        for x in range(half):
            for y in range(half):
                up = lifted[oz, x * half + y]
                for xx in range(2):
                    for yy in range(2):
                        value = enc[s, 2 * x + xx, 2 * y + yy] + up
                        table[s, 2 * x + xx, 2 * y + yy] = value.astype(BF16).astype(F32)
        stage_faces(face_out2, s)
    halo2 = face_copies(face_out2, face_in2, 1)
    start_pair(halo2[0], has_next, halo2[1], has_prev)
    loads[4].wait()
    finish_pair(halo2[0], has_next, halo2[1], has_prev)
    take_faces(face_in2)

    @pl.loop(0, slots)
    def _(b):
        out_ref[b] = convolve(table, below, above, fine_index(b), w4)


def per_device(
    n,
    features,
    fine_nbr,
    fine_send,
    fine_parent,
    coarse_child,
    coarse_nbr,
    enc_fine_w,
    enc_coarse_w,
    dec_coarse_w,
    dec_fine_w,
):
    slots, edge, width = features.shape[0], features.shape[1], features.shape[-1]
    per = coarse_nbr.shape[0]
    bricks = LANES * per
    half = edge // 2
    plane = edge * edge
    voxels = edge**3
    rows = -(-2 * per // 8) * 8
    kernels = [
        w.reshape(3, 9 * width, width)
        for w in (enc_fine_w, enc_coarse_w, dec_coarse_w, dec_fine_w)
    ]
    vmem = pltpu.VMEM
    smem_spec = pl.BlockSpec(memory_space=pltpu.SMEM)
    vmem_spec = pl.BlockSpec(memory_space=pltpu.VMEM)
    any_spec = pl.BlockSpec(memory_space=pl.ANY)
    cube = (edge, edge, edge, width)
    face = (edge, edge, width)
    dma = pltpu.SemaphoreType.DMA
    out = pl.pallas_call(
        functools.partial(kernel, n),
        out_shape=jax.ShapeDtypeStruct((slots, voxels, width), BF16),
        in_specs=[smem_spec] * 3 + [vmem_spec] * 2 + [any_spec] * 5,
        out_specs=vmem_spec,
        scratch_shapes=[
            vmem((slots, voxels, width), BF16),
            *[vmem((3, 9 * width, width), BF16)] * 4,
            vmem((edge + 2, edge + 2, 3 * edge, width), F32),
            vmem(((edge + 2) * plane, 9 * width), BF16),
            vmem((slots + 1,) + cube, F32),
            vmem((slots,) + cube, F32),
            vmem((slots + 1,) + face, F32),
            vmem((slots + 1,) + face, F32),
            vmem((2, slots, plane, width), BF16),
            vmem((2, slots, plane, width), BF16),
            vmem((2, slots, plane, width), BF16),
            vmem((2, slots, plane, width), BF16),
            vmem((half * half * edge, width), F32),
            vmem((LANES, slots, half**3, width), BF16),
            vmem((LANES * slots + 1, half**3, width), F32),
            vmem((LANES, rows, 128), jnp.int32),
            pltpu.SMEM((LANES, rows, 128), jnp.int32),
            vmem((bricks + 1,) + cube, F32),
            vmem((bricks + 1,) + cube, F32),
            vmem((bricks + 1,) + cube, F32),
            vmem((3 * bricks + 1,) + face, F32),
            vmem((3 * bricks + 1,) + face, F32),
            vmem((bricks, 2, plane, width), BF16),
            vmem((2, bricks, 2, plane, width), BF16),
            vmem((bricks, 2, plane, width), BF16),
            vmem((2, bricks, 2, plane, width), BF16),
            vmem((half * half * 2 * edge, width), F32),
            vmem((2, half * half, edge, width), F32),
            dma((5,)),
            dma((2, 2)),
            dma((2, 2)),
            dma((LANES - 1, slots)),
            dma((LANES - 1, slots)),
            dma((LANES - 1,)),
            dma((LANES - 1,)),
            dma((2, 2)),
            dma((2, 2)),
            dma(()),
        ],
        compiler_params=pltpu.CompilerParams(
            collective_id=0, has_side_effects=True, vmem_limit_bytes=60 * 1024 * 1024
        ),
    )(
        fine_nbr,
        fine_send[0],
        fine_parent,
        coarse_child,
        coarse_nbr,
        features.reshape(slots, voxels, width),
        *kernels,
    )
    return out.reshape(features.shape)


def solution(mesh):
    lead = ("groups", "gx")
    placed = (
        P(lead, None, None, None, None),
        P(lead, None),
        P(lead, None, None),
        P(lead),
        P(lead, None),
        P(lead, None),
        P(),
        P(),
        P(),
        P(),
    )
    return jax.shard_map(
        functools.partial(per_device, mesh.shape["gx"]),
        mesh=mesh,
        in_specs=placed,
        out_specs=P(lead, None, None, None, None),
        check_vma=False,
    )
```

profile of v0, /device:TPU:1, one launch (start us, length us, event | category | flops | bytes accessed | tf_op | source)
XLA Modules:
  0.0 45.7 jit_solution(3365675577354694762)
XLA Ops:
  0.0 43.8 %shard_map.100 = bf16[4,512,128]{2,1,0:T(8,128)(2,1)} custom-call(s32[4,27]{1,0:T(4,128)} %fine_nbr.1, s32[2,4]{1,0:T(2,128)} %bitcast.13, s32[4]{0:T(128)} %fine_parent.1, s32[1,8]{1,0:T(1,128)} %child_ref.1, s32[1,27]{1,0:T(1,128)} %nbr_ref.1, bf16[4,512,128]{2,1,0:T(8,128)(2,1)} %bitcast.12, bf16[3,1152,128]{2,1,0:T(8,128)(2,1)} %bitcast.8, ...), custom_call_target="tpu_custom_call" | custom-call | tf_op jit(solution)/shard_map/pallas_call | solution.py:441
  43.8 1.9 %copy.12 = bf16[4,8,8,8,128]{4,3,2,1,0:T(8,128)(2,1)} copy(bf16[4,8,8,8,128]{4,3,2,1,0:T(8,128)(2,1)} %bitcast.7) | data formatting | bytes 1048576
where the time goes:
time: 45.9 us; the launch traced here: 45.7 us
  Pallas kernels  43.8 us (95%)
  local copies, waits for them, and re-layouts  1.87 us (4%)
    pallas_call x1, Pallas kernels, per_device(): pl.pallas_call(functools.partial(kernel, n), out_shape=jax.ShapeDtypeStru...  43.8 us
    unnamed x1, local copies, waits for them, and re-layouts  1.87 us

commit v1 on v0

--- a/solution.py
+++ b/solution.py
@@ -64,7 +64,6 @@
     meta_s,
     coarse,
     coarse2,
-    coarse3,
     low_x,
     high_x,
     side_out,
@@ -98,14 +97,26 @@
     def peer(k):
         return me - member + (member ^ k)
 
-    loads = [
-        pltpu.make_async_copy(src, dst, load_sem.at[i])
-        for i, (src, dst) in enumerate(
-            ((feat_hbm, feat), (w1_hbm, w1), (w2_hbm, w2), (w3_hbm, w3), (w4_hbm, w4))
-        )
-    ]
-    for copy in loads:
-        copy.start()
+    width = out_ref.shape[-1]
+    loads = [[pltpu.make_async_copy(feat_hbm, feat, load_sem.at[0, 0])]]
+    for i, (src, dst) in enumerate(
+        ((w1_hbm, w1), (w2_hbm, w2), (w3_hbm, w3), (w4_hbm, w4))
+    ):
+        loads.append(
+            [
+                pltpu.make_async_copy(
+                    src.at[dx], dst.at[:, dx * width : (dx + 1) * width], load_sem.at[i + 1, dx]
+                )
+                for dx in range(3)
+            ]
+        )
+    for copies in loads:
+        for copy in copies:
+            copy.start()
+
+    def loaded(i):
+        for copy in loads[i]:
+            copy.wait()
 
     has_prev, has_next = me > 0, me < n - 1
     has_down, has_up = me >= LANES, me < n - LANES
@@ -184,7 +195,7 @@
         outgoing[0, s] = table[up_from, edge - 1].reshape(plane, width).astype(BF16)
         outgoing[1, s] = table[down_from, 0].reshape(plane, width).astype(BF16)
 
-    loads[0].wait()
+    loaded(0)
     for s in range(slots):
         table[s] = feat[s].astype(F32).reshape(cube)
     for s in range(slots):
@@ -208,14 +219,13 @@
     above[slots] = zero_plane
     coarse[bricks] = zero_brick
     coarse2[bricks] = zero_brick
-    coarse3[bricks] = zero_brick
     low_x[3 * bricks] = zero_plane
     high_x[3 * bricks] = zero_plane
     children[LANES * slots] = jnp.zeros((block, width), F32)
 
     base = edge
 
-    def convolve(centre, lower, upper, index, weights):
+    def assemble(centre, lower, upper, index):
         for t in range(27):
             dx, dy, dz = t // 9 - 1, t // 3 % 3 - 1, t % 3 - 1
             at = index(t)
@@ -227,6 +237,23 @@
             else:
                 piece = upper[at, ys, zs, :][None]
             pad[place(dx, edge, 1), place(dy, edge, 1), place(dz, edge, base), :] = piece
+
+    def product(weights, planes, rows):
+        two = jnp.dot(
+            cols[0 : (planes + 1) * rows, :],
+            weights[:, 0 : 2 * width],
+            preferred_element_type=F32,
+        )
+        third = jnp.dot(
+            cols[2 * rows : (planes + 2) * rows, :],
+            weights[:, 2 * width : 3 * width],
+            preferred_element_type=F32,
+        )
+        total = third + two[0 : planes * rows, 0:width] + two[rows:, width : 2 * width]
+        return jnp.maximum(total, 0.0).astype(BF16)
+
+    def convolve(centre, lower, upper, index, weights):
+        assemble(centre, lower, upper, index)
         for x in range(edge + 2):
             for k in range(9):
                 dy, dz = k // 3, k % 3 - 1
@@ -234,15 +261,7 @@
                 cols[x * plane : (x + 1) * plane, k * width : (k + 1) * width] = piece.reshape(
                     plane, width
                 ).astype(BF16)
-        total = None
-        for dx in range(3):
-            part = jnp.dot(
-                cols[dx * plane : (dx + edge) * plane, :],
-                weights[dx],
-                preferred_element_type=F32,
-            )
-            total = part if total is None else total + part
-        return jnp.maximum(total, 0.0).astype(BF16)
+        return product(weights, edge, plane)
 
     def fine_index(b):
         def index(t):
@@ -258,7 +277,7 @@
 
     finish_pair(halo1[0], has_next, halo1[1], has_prev)
     take_faces(face_in)
-    loads[1].wait()
+    loaded(1)
 
     def pool_copy(k, b):
         return remote(
@@ -331,22 +350,21 @@
         )
         return up, down
 
-    def coarse_index(j):
-        lane, slot = lax.div(j, per), lax.rem(j, per)
-
+    def coarse_index(lane, slot, live):
         def index(t):
             value = meta_s[lane, per + slot, t]
+            there = (value >= 0) & live
             device, at = owner_of(value)
             at = lax.rem(device, LANES) * per + at
             if t // 9 == 1:
-                return jnp.where(value >= 0, at, bricks)
+                return jnp.where(there, at, bricks)
             at = at + (lax.div(device, LANES) - group + 1) * bricks
             at = jnp.minimum(jnp.maximum(at, 0), 3 * bricks)
-            return jnp.where(value >= 0, at, 3 * bricks)
+            return jnp.where(there, at, 3 * bricks)
 
         return index
 
-    def coarse_layer(source, target, outgoing, incoming, phase, weights):
+    def exchange_sides(source, outgoing, incoming, phase):
         for j in range(bricks):
             first, last = source[j, 0], source[j, edge - 1]
             low_x[bricks + j] = first
@@ -361,27 +379,46 @@
                 low_x[start + j] = incoming[side, j, 0].astype(F32).reshape(edge, edge, width)
                 high_x[start + j] = incoming[side, j, 1].astype(F32).reshape(edge, edge, width)
 
-        @pl.loop(0, bricks)
-        def _(j):
-            value = convolve(source, high_x, low_x, coarse_index(j), weights)
-            target[j] = value.astype(F32).reshape(cube)
-
-    loads[2].wait()
-    coarse_layer(coarse, coarse2, side_out, side_in, 0, w2)
-    loads[3].wait()
-    coarse_layer(coarse2, coarse3, side_out2, side_in2, 1, w3)
-
-    for s in range(slots):
+    exchange_sides(coarse, side_out, side_in, 0)
+    loaded(2)
+
+    @pl.loop(0, bricks)
+    def _(j):
+        lane, slot = lax.div(j, per), lax.rem(j, per)
+        value = convolve(coarse, high_x, low_x, coarse_index(lane, slot, True), w2)
+        coarse2[j] = value.astype(F32).reshape(cube)
+
+    exchange_sides(coarse2, side_out2, side_in2, 1)
+    loaded(3)
+
+    part = half * edge
+    strip = slots * part
+
+    @pl.loop(0, slots)
+    def _(s):
         parent = fine_parent[s]
         safe = jnp.maximum(parent, 0)
-        device, at = owner_of(lax.div(safe, 8))
-        at = jnp.where(parent >= 0, lax.rem(device, LANES) * per + at, bricks)
+        device, slot = owner_of(lax.div(safe, 8))
         octant = lax.rem(safe, 8)
-        ox = lax.div(octant, 4)
-        oy = lax.rem(lax.div(octant, 2), 2)
-        oz = lax.rem(octant, 2)
-        piece = coarse3[at, pl.ds(ox * half, half), pl.ds(oy * half, half), :, :]
-        piece = piece.reshape(half * half * edge, width)
+        ox = lax.div(octant, 4) * half
+        oy = lax.rem(lax.div(octant, 2), 2) * half
+        assemble(
+            coarse2, high_x, low_x, coarse_index(lax.rem(device, LANES), slot, parent >= 0)
+        )
+        for x in range(half + 2):
+            start = pl.multiple_of(x * strip + s * part, part)
+            for k in range(9):
+                dy, dz = k // 3, k % 3 - 1
+                piece = pad[ox + x, pl.ds(oy + dy, half), base + dz : base + dz + edge, :]
+                cols[pl.ds(start, part), k * width : (k + 1) * width] = piece.reshape(
+                    part, width
+                ).astype(BF16)
+
+    parents = product(w3, half, strip).astype(F32).reshape(half, slots, part, width)
+
+    for s in range(slots):
+        oz = lax.rem(jnp.maximum(fine_parent[s], 0), 2)
+        piece = parents[:, s].reshape(half * half * edge, width)
         spread[pl.ds(0, half * half * edge, stride=2), :] = piece
         spread[pl.ds(1, half * half * edge, stride=2), :] = piece
         for z in range(2):
@@ -398,7 +435,7 @@
         stage_faces(face_out2, s)
     halo2 = face_copies(face_out2, face_in2, 1)
     start_pair(halo2[0], has_next, halo2[1], has_prev)
-    loads[4].wait()
+    loaded(4)
     finish_pair(halo2[0], has_next, halo2[1], has_prev)
     take_faces(face_in2)
 
@@ -426,6 +463,7 @@
     half = edge // 2
     plane = edge * edge
     voxels = edge**3
+    strip = slots * half * edge
     rows = -(-2 * per // 8) * 8
     kernels = [
         w.reshape(3, 9 * width, width)
@@ -445,9 +483,9 @@
         out_specs=vmem_spec,
         scratch_shapes=[
             vmem((slots, voxels, width), BF16),
-            *[vmem((3, 9 * width, width), BF16)] * 4,
+            *[vmem((9 * width, 3 * width), BF16)] * 4,
             vmem((edge + 2, edge + 2, 3 * edge, width), F32),
-            vmem(((edge + 2) * plane, 9 * width), BF16),
+            vmem((max((edge + 2) * plane, (half + 2) * strip), 9 * width), BF16),
             vmem((slots + 1,) + cube, F32),
             vmem((slots,) + cube, F32),
             vmem((slots + 1,) + face, F32),
@@ -463,7 +501,6 @@
             pltpu.SMEM((LANES, rows, 128), jnp.int32),
             vmem((bricks + 1,) + cube, F32),
             vmem((bricks + 1,) + cube, F32),
-            vmem((bricks + 1,) + cube, F32),
             vmem((3 * bricks + 1,) + face, F32),
             vmem((3 * bricks + 1,) + face, F32),
             vmem((bricks, 2, plane, width), BF16),
@@ -472,7 +509,7 @@
             vmem((2, bricks, 2, plane, width), BF16),
             vmem((half * half * 2 * edge, width), F32),
             vmem((2, half * half, edge, width), F32),
-            dma((5,)),
+            dma((5, 3)),
             dma((2, 2)),
             dma((2, 2)),
             dma((LANES - 1, slots)),

time: 45.9 us -> 40.2 us (0.88)
  Pallas kernels: 43.8 us -> 38.1 us
    pallas_call x1, Pallas kernels: 43.8 us -> 38.1 us  [per_device(): pl.pallas_call(functools.partial(kernel, n), out_shape=jax.ShapeDtypeStru...]
where the time goes in v1:
time: 40.2 us; the launch traced here: 40 us
  Pallas kernels  38.1 us (95%)
  local copies, waits for them, and re-layouts  1.87 us (5%)
    pallas_call x1, Pallas kernels, per_device(): pl.pallas_call(functools.partial(kernel, n), out_shape=jax.ShapeDtypeStru...  38.1 us
    unnamed x1, local copies, waits for them, and re-layouts  1.87 us

profile of v1, /device:TPU:1, one launch (start us, length us, event | category | flops | bytes accessed | tf_op | source)
XLA Modules:
  0.0 40.0 jit_solution(1784681420922371800)
XLA Ops:
  0.0 38.1 %shard_map.100 = bf16[4,512,128]{2,1,0:T(8,128)(2,1)} custom-call(s32[4,27]{1,0:T(4,128)} %fine_nbr.1, s32[2,4]{1,0:T(2,128)} %bitcast.13, s32[4]{0:T(128)} %fine_parent.1, s32[1,8]{1,0:T(1,128)} %child_ref.1, s32[1,27]{1,0:T(1,128)} %nbr_ref.1, bf16[4,512,128]{2,1,0:T(8,128)(2,1)} %bitcast.12, bf16[3,1152,128]{2,1,0:T(8,128)(2,1)} %bitcast.8, ...), custom_call_target="tpu_custom_call" | custom-call | tf_op jit(solution)/shard_map/pallas_call | solution.py:479
  38.1 1.9 %copy.12 = bf16[4,8,8,8,128]{4,3,2,1,0:T(8,128)(2,1)} copy(bf16[4,8,8,8,128]{4,3,2,1,0:T(8,128)(2,1)} %bitcast.7) | data formatting | bytes 1048576

commit v2 on v1

--- a/solution.py
+++ b/solution.py
@@ -49,6 +49,7 @@
     w4,
     pad,
     cols,
+    opened,
     table,
     enc,
     below,
@@ -225,8 +226,8 @@
 
     base = edge
 
-    def assemble(centre, lower, upper, index):
-        for t in range(27):
+    def assemble(centre, lower, upper, index, taps=range(27)):
+        for t in taps:
             dx, dy, dz = t // 9 - 1, t // 3 % 3 - 1, t % 3 - 1
             at = index(t)
             ys, zs = pick(dy, edge), pick(dz, edge)
@@ -262,6 +263,53 @@
                     plane, width
                 ).astype(BF16)
         return product(weights, edge, plane)
+
+    own_taps = range(9, 18)
+    far_taps = (*range(9), *range(18, 27))
+
+    def gather_columns(x, row):
+        for k in range(9):
+            dy, dz = k // 3, k % 3 - 1
+            piece = pad[x, dy : dy + edge, base + dz : base + dz + edge, :]
+            cols[pl.ds(row, plane), k * width : (k + 1) * width] = piece.reshape(
+                plane, width
+            ).astype(BF16)
+
+    def local_product(centre, j, index, weights):
+        assemble(centre, None, None, index, own_taps)
+        for x in range(edge):
+            gather_columns(x + 1, x * plane)
+        two = jnp.dot(
+            cols[0 : edge * plane, :], weights[:, 0 : 2 * width], preferred_element_type=F32
+        )
+        third = jnp.dot(
+            cols[plane : edge * plane, :],
+            weights[:, 2 * width : 3 * width],
+            preferred_element_type=F32,
+        )
+        inner = slice(plane, (edge - 1) * plane)
+        middle = two[:, width : 2 * width]
+        opened[j, 0] = middle[0:plane] + third[0:plane]
+        opened[j, 1] = middle[(edge - 1) * plane :] + two[(edge - 2) * plane : (edge - 1) * plane, 0:width]
+        total = middle[inner] + third[inner] + two[0 : (edge - 2) * plane, 0:width]
+        return jnp.maximum(total, 0.0).astype(BF16)
+
+    def outer_planes(count, lower, upper, index_of, weights, store):
+        @pl.loop(0, count)
+        def _(j):
+            assemble(None, lower, upper, index_of(j), far_taps)
+            gather_columns(0, pl.multiple_of(j * plane, plane))
+            gather_columns(edge + 1, pl.multiple_of((count + j) * plane, plane))
+
+        for side in range(2):
+            added = jnp.dot(
+                cols[side * count * plane : (side + 1) * count * plane, :],
+                weights[:, 2 * side * width : (2 * side + 1) * width],
+                preferred_element_type=F32,
+            )
+            for j in range(count):
+                total = opened[j, side] + added[j * plane : (j + 1) * plane]
+                store(j, side * (edge - 1), jnp.maximum(total, 0.0).astype(BF16))
 
     def fine_index(b):
         def index(t):
@@ -364,7 +412,7 @@
 
         return index
 
-    def exchange_sides(source, outgoing, incoming, phase):
+    def send_sides(source, outgoing, incoming, phase):
         for j in range(bricks):
             first, last = source[j, 0], source[j, edge - 1]
             low_x[bricks + j] = first
@@ -373,39 +421,49 @@
             outgoing[j, 1] = last.reshape(plane, width).astype(BF16)
         up, down = side_copies(outgoing, incoming, phase)
         start_pair(up, has_up, down, has_down)
-        finish_pair(up, has_up, down, has_down)
+        return up, down
+
+    def take_sides(copies, incoming):
+        finish_pair(copies[0], has_up, copies[1], has_down)
         for side, start in ((0, 0), (1, 2 * bricks)):
             for j in range(bricks):
                 low_x[start + j] = incoming[side, j, 0].astype(F32).reshape(edge, edge, width)
                 high_x[start + j] = incoming[side, j, 1].astype(F32).reshape(edge, edge, width)
 
-    exchange_sides(coarse, side_out, side_in, 0)
+    def group_index(j):
+        return coarse_index(lax.div(j, per), lax.rem(j, per), True)
+
+    face = (edge, edge, width)
+    copies = send_sides(coarse, side_out, side_in, 0)
     loaded(2)
 
     @pl.loop(0, bricks)
     def _(j):
-        lane, slot = lax.div(j, per), lax.rem(j, per)
-        value = convolve(coarse, high_x, low_x, coarse_index(lane, slot, True), w2)
-        coarse2[j] = value.astype(F32).reshape(cube)
-
-    exchange_sides(coarse2, side_out2, side_in2, 1)
+        value = local_product(coarse, j, group_index(j), w2).astype(F32)
+        coarse2[j, 1 : edge - 1] = value.reshape((edge - 2,) + face)
+
+    take_sides(copies, side_in)
+
+    def store_coarse(j, x, value):
+        coarse2[j, x] = value.astype(F32).reshape(face)
+
+    outer_planes(bricks, high_x, low_x, group_index, w2, store_coarse)
+    copies = send_sides(coarse2, side_out2, side_in2, 1)
     loaded(3)
 
     part = half * edge
     strip = slots * part
 
-    @pl.loop(0, slots)
-    def _(s):
+    def quarter(s, taps, planes):
         parent = fine_parent[s]
         safe = jnp.maximum(parent, 0)
         device, slot = owner_of(lax.div(safe, 8))
         octant = lax.rem(safe, 8)
         ox = lax.div(octant, 4) * half
         oy = lax.rem(lax.div(octant, 2), 2) * half
-        assemble(
-            coarse2, high_x, low_x, coarse_index(lax.rem(device, LANES), slot, parent >= 0)
-        )
-        for x in range(half + 2):
+        index = coarse_index(lax.rem(device, LANES), slot, parent >= 0)
+        assemble(coarse2, high_x, low_x, index, taps)
+        for x in planes:
             start = pl.multiple_of(x * strip + s * part, part)
             for k in range(9):
                 dy, dz = k // 3, k % 3 - 1
@@ -413,6 +471,16 @@
                 cols[pl.ds(start, part), k * width : (k + 1) * width] = piece.reshape(
                     part, width
                 ).astype(BF16)
+
+    @pl.loop(0, slots)
+    def _(s):
+        quarter(s, own_taps, range(1, half + 1))
+
+    take_sides(copies, side_in2)
+
+    @pl.loop(0, slots)
+    def _(s):
+        quarter(s, range(27), (0, half + 1))
 
     parents = product(w3, half, strip).astype(F32).reshape(half, slots, part, width)
 
@@ -436,12 +504,19 @@
     halo2 = face_copies(face_out2, face_in2, 1)
     start_pair(halo2[0], has_next, halo2[1], has_prev)
     loaded(4)
+
+    @pl.loop(0, slots)
+    def _(b):
+        value = local_product(table, b, fine_index(b), w4)
+        out_ref[b, plane : (edge - 1) * plane, :] = value
+
     finish_pair(halo2[0], has_next, halo2[1], has_prev)
     take_faces(face_in2)
 
-    @pl.loop(0, slots)
-    def _(b):
-        out_ref[b] = convolve(table, below, above, fine_index(b), w4)
+    def store_fine(b, x, value):
+        out_ref[b, x * plane : (x + 1) * plane, :] = value
+
+    outer_planes(slots, below, above, fine_index, w4, store_fine)
 
 
 def per_device(
@@ -485,7 +560,8 @@
             vmem((slots, voxels, width), BF16),
             *[vmem((9 * width, 3 * width), BF16)] * 4,
             vmem((edge + 2, edge + 2, 3 * edge, width), F32),
-            vmem((max((edge + 2) * plane, (half + 2) * strip), 9 * width), BF16),
+            vmem((max((edge + 2) * plane, (half + 2) * strip, 2 * max(slots, bricks) * plane), 9 * width), BF16),
+            vmem((max(slots, bricks), 2, plane, width), F32),
             vmem((slots + 1,) + cube, F32),
             vmem((slots,) + cube, F32),
             vmem((slots + 1,) + face, F32),

time: 40.2 us -> 34.4 us (0.86)
  Pallas kernels: 38.1 us -> 32.1 us
    pallas_call x1, Pallas kernels: 38.1 us -> 32.1 us  [per_device(): pl.pallas_call(functools.partial(kernel, n), out_shape=jax.ShapeDtypeStru...]
where the time goes in v2:
time: 34.4 us; the launch traced here: 34 us
  Pallas kernels  32.1 us (93%)
  local copies, waits for them, and re-layouts  1.87 us (5%)
    pallas_call x1, Pallas kernels, per_device(): pl.pallas_call(functools.partial(kernel, n), out_shape=jax.ShapeDtypeStru...  32.1 us
    unnamed x1, local copies, waits for them, and re-layouts  1.87 us

profile of v2, /device:TPU:1, one launch (start us, length us, event | category | flops | bytes accessed | tf_op | source)
XLA Modules:
  0.0 34.0 jit_solution(17310152733878031146)
XLA Ops:
  0.0 32.1 %shard_map.100 = bf16[4,512,128]{2,1,0:T(8,128)(2,1)} custom-call(s32[4,27]{1,0:T(4,128)} %fine_nbr.1, s32[2,4]{1,0:T(2,128)} %bitcast.13, s32[4]{0:T(128)} %fine_parent.1, s32[1,8]{1,0:T(1,128)} %child_ref.1, s32[1,27]{1,0:T(1,128)} %nbr_ref.1, bf16[4,512,128]{2,1,0:T(8,128)(2,1)} %bitcast.12, bf16[3,1152,128]{2,1,0:T(8,128)(2,1)} %bitcast.8, ...), custom_call_target="tpu_custom_call" | custom-call | tf_op jit(solution)/shard_map/pallas_call | solution.py:554
  32.1 1.9 %copy.12 = bf16[4,8,8,8,128]{4,3,2,1,0:T(8,128)(2,1)} copy(bf16[4,8,8,8,128]{4,3,2,1,0:T(8,128)(2,1)} %bitcast.7) | data formatting | bytes 1048576

commit v3 on v2

--- a/solution.py
+++ b/solution.py
@@ -60,6 +60,7 @@
     face_in2,
     half_z,
     pooled,
+    pooled_out,
     children,
     meta,
     meta_s,
@@ -253,17 +254,6 @@
         total = third + two[0 : planes * rows, 0:width] + two[rows:, width : 2 * width]
         return jnp.maximum(total, 0.0).astype(BF16)
 
-    def convolve(centre, lower, upper, index, weights):
-        assemble(centre, lower, upper, index)
-        for x in range(edge + 2):
-            for k in range(9):
-                dy, dz = k // 3, k % 3 - 1
-                piece = pad[x, dy : dy + edge, base + dz : base + dz + edge, :]
-                cols[x * plane : (x + 1) * plane, k * width : (k + 1) * width] = piece.reshape(
-                    plane, width
-                ).astype(BF16)
-        return product(weights, edge, plane)
-
     own_taps = range(9, 18)
     far_taps = (*range(9), *range(18, 27))
 
@@ -323,43 +313,63 @@
             below[s] = incoming[0, s].astype(F32).reshape(edge, edge, width)
             above[s] = incoming[1, s].astype(F32).reshape(edge, edge, width)
 
+    loaded(1)
+    face = (edge, edge, width)
+    cells = half * half
+
+    def pool_copy(k, b):
+        if b is None:
+            source, at = pooled_out.at[member], slots
+        else:
+            source, at = pooled.at[member, b], b
+        return remote(
+            source, source, pool_send_sem.at[k - 1, at], pool_recv_sem.at[k - 1, at], peer(k)
+        )
+
+    def pool(value, count):
+        pairs = value.reshape(count, 2, half, 2, edge, width)
+        summed = (pairs[:, 0, :, 0] + pairs[:, 0, :, 1]) + (pairs[:, 1, :, 0] + pairs[:, 1, :, 1])
+        half_z[0 : count * half * edge, :] = summed.reshape(count * half * edge, width)
+        even = half_z[pl.ds(0, count * cells, stride=2), :]
+        odd = half_z[pl.ds(1, count * cells, stride=2), :]
+        return ((even + odd) * 0.125).astype(BF16)
+
+    @pl.loop(0, slots)
+    def _(b):
+        value = local_product(table, b, fine_index(b), w1).astype(F32)
+        value = value.reshape((edge - 2,) + face)
+        enc[b, 1 : edge - 1] = value
+        pooled[member, b] = pool(value[1 : edge - 3], half - 2)
+        for k in range(1, LANES):
+            pool_copy(k, b).start()
+
     finish_pair(halo1[0], has_next, halo1[1], has_prev)
     take_faces(face_in)
-    loaded(1)
-
-    def pool_copy(k, b):
-        return remote(
-            pooled.at[member, b],
-            pooled.at[member, b],
-            pool_send_sem.at[k - 1, b],
-            pool_recv_sem.at[k - 1, b],
-            peer(k),
-        )
-
-    @pl.loop(0, slots)
-    def _(b):
-        value = convolve(table, below, above, fine_index(b), w1).astype(F32).reshape(cube)
-        enc[b] = value
-        pairs = value.reshape(half, 2, half, 2, edge, width)
-        summed = (pairs[:, 0, :, 0] + pairs[:, 0, :, 1]) + (pairs[:, 1, :, 0] + pairs[:, 1, :, 1])
-        half_z[...] = summed.reshape(half * half * edge, width)
-        even = half_z[pl.ds(0, block, stride=2), :]
-        odd = half_z[pl.ds(1, block, stride=2), :]
-        pooled[member, b] = ((even + odd) * 0.125).astype(BF16)
-        for k in range(1, LANES):
-            pool_copy(k, b).start()
+
+    def store_enc(b, x, value):
+        enc[b, x] = value.astype(F32).reshape(face)
+
+    outer_planes(slots, below, above, fine_index, w1, store_enc)
+    for b in range(slots):
+        pooled_out[member, b, 0:cells] = pool(enc[b, 0:2], 1)
+        pooled_out[member, b, cells : 2 * cells] = pool(enc[b, edge - 2 : edge], 1)
+    for k in range(1, LANES):
+        pool_copy(k, None).start()
 
     for copy in meta_copies:
         copy.wait()
     to_smem = pltpu.make_async_copy(meta, meta_s, meta_sem)
     to_smem.start()
     for k in range(1, LANES):
-        for b in range(slots):
+        for b in (*range(slots), None):
             pool_copy(k, b).wait()
     to_smem.wait()
     for lane in range(LANES):
         for s in range(slots):
-            children[lane * slots + s] = pooled[lane, s].astype(F32)
+            at = lane * slots + s
+            children[at, cells : block - cells] = pooled[lane, s].astype(F32)
+            children[at, 0:cells] = pooled_out[lane, s, 0:cells].astype(F32)
+            children[at, block - cells : block] = pooled_out[lane, s, cells : 2 * cells].astype(F32)
 
     def owner_of(value):
         value = jnp.maximum(value, 0)
@@ -571,7 +581,8 @@
             vmem((2, slots, plane, width), BF16),
             vmem((2, slots, plane, width), BF16),
             vmem((half * half * edge, width), F32),
-            vmem((LANES, slots, half**3, width), BF16),
+            vmem((LANES, slots, (half - 2) * half**2, width), BF16),
+            vmem((LANES, slots, 2 * half**2, width), BF16),
             vmem((LANES * slots + 1, half**3, width), F32),
             vmem((LANES, rows, 128), jnp.int32),
             pltpu.SMEM((LANES, rows, 128), jnp.int32),
@@ -588,8 +599,8 @@
             dma((5, 3)),
             dma((2, 2)),
             dma((2, 2)),
-            dma((LANES - 1, slots)),
-            dma((LANES - 1, slots)),
+            dma((LANES - 1, slots + 1)),
+            dma((LANES - 1, slots + 1)),
             dma((LANES - 1,)),
             dma((LANES - 1,)),
             dma((2, 2)),

time: 34.4 us -> 33 us (0.959)
  the two profiles are of different devices: /device:TPU:1 before, /device:TPU:0 now
where the time goes in v3:
time: 33 us; the launch traced here: 32.8 us
  Pallas kernels  30.9 us (94%)
  local copies, waits for them, and re-layouts  1.87 us (6%)
    pallas_call x1, Pallas kernels, per_device(): pl.pallas_call(functools.partial(kernel, n), out_shape=jax.ShapeDtypeStru...  30.9 us
    unnamed x1, local copies, waits for them, and re-layouts  1.87 us

profile of v3, /device:TPU:0, one launch (start us, length us, event | category | flops | bytes accessed | tf_op | source)
XLA Modules:
  0.0 32.8 jit_solution(11405709841191604001)
XLA Ops:
  0.0 30.9 %shard_map.100 = bf16[4,512,128]{2,1,0:T(8,128)(2,1)} custom-call(s32[4,27]{1,0:T(4,128)} %fine_nbr.1, s32[2,4]{1,0:T(2,128)} %bitcast.13, s32[4]{0:T(128)} %fine_parent.1, s32[1,8]{1,0:T(1,128)} %child_ref.1, s32[1,27]{1,0:T(1,128)} %nbr_ref.1, bf16[4,512,128]{2,1,0:T(8,128)(2,1)} %bitcast.12, bf16[3,1152,128]{2,1,0:T(8,128)(2,1)} %bitcast.8, ...), custom_call_target="tpu_custom_call" | custom-call | tf_op jit(solution)/shard_map/pallas_call | solution.py:564
  30.9 1.9 %copy.12 = bf16[4,8,8,8,128]{4,3,2,1,0:T(8,128)(2,1)} copy(bf16[4,8,8,8,128]{4,3,2,1,0:T(8,128)(2,1)} %bitcast.7) | data formatting | bytes 1048576
